TPU v7x, 32 devices: a whole 2x2x4 slice. The times are simulated.
32 devices in a mesh: groups: 2 (over y), tm: 4 (over z), space: 2 (over x), clip: 2 (over core).
Axes of the slice: x: 2, y: 2, z: 4, core: 2. Of those that a mesh axis runs over, the one named last changes fastest.
Arguments:
- features: bfloat16 [4, 16, 8, 16, 256], P(('groups', 'clip'), 'tm', 'space'), parts along dimension 0, may hold values from -6 to 6
- frame_counts: int32 [4], P(('groups', 'clip')), parts along dimension 0, may hold values from 1 to 16, as said below
- routes: int32 [4, 512, 1], P(('groups', 'clip'), ('tm', 'space')), parts along dimension 0, may hold values from 0 to 7; in each aligned block of 64 rows (0 to 63, 64 to 127, ..., all dimensions but the last counted through in order) at most 9 rows name the same one
- norm_gains: float32 [3, 256], replicated, may hold values from 0.5 to 1.5
- conv_weights: bfloat16 [2, 256, 27, 256], P(None, 'tm'), may hold values from -0.078125 to 0.078125
- conv_biases: float32 [2, 256], replicated, may hold values from -3 to 3
- latent_weight: bfloat16 [256, 16], replicated, may hold values from -0.375 to 0.375
- embed_weight: bfloat16 [64, 3072], replicated, may hold values from -0.75 to 0.75
- embed_bias: float32 [3072], replicated, may hold values from -3 to 3
Outputs:
- packed: bfloat16 [4, 576, 3072], P(('groups', 'clip'), ('tm', 'space')), parts along dimension 0
There are 2 independent parts, one for each index of `groups`. A program takes and returns all parts, laid end to end along the dimension named above; an argument that names none is the same for every part. Nothing has to cross between parts.
Inputs may be any that keep to these rules, and one draw needn't show every extreme that they name: `routes`: in each clip, the 64 patches of one span and tile name any one owner at most 9 times. `frame_counts`: one clip of each part has all 16 frames valid.
All inputs are finite; a program needn't handle non-finite values.
Results may differ from a plain program's by a relative error of at most 0.0054.
Values may be sent and summed in bfloat16 or wider, within the bound.
A program may use at most 64 MiB of HBM per device.

v0:
```python
import jax
import jax.numpy as jnp
from jax import lax
from jax.sharding import PartitionSpec as P


def shifted(block, axis, distance):
    devices = range(lax.axis_size(axis))
    route = [(i - distance, i) for i in devices if i - distance in devices]
    return lax.ppermute(block, axis, route)


def with_halo(cells, sides, width):
    for axis, dim in sides:
        count = lax.axis_size(axis)
        ends = count - 1
        head = lax.slice_in_dim(cells, 0, width, axis=dim)
        tail = lax.slice_in_dim(cells, cells.shape[dim] - width, cells.shape[dim], axis=dim)
        cells = jnp.concatenate(
            [
                lax.ppermute(tail, axis, [(i, (i + 1) % count) for i in range(ends)]),
                cells,
                lax.ppermute(head, axis, [((i + 1) % count, i) for i in range(ends)]),
            ],
            axis=dim,
        )
    return cells


def norm_silu(values, gain):
    scale = lax.rsqrt(jnp.mean(values * values, axis=-1, keepdims=True) + 1e-06)
    return jax.nn.silu(values * scale * gain)


def conv_taps(padded, weights):
    frames = padded.shape[0] - 2
    rows = padded.shape[1] - 2
    cols = padded.shape[2] - 2
    inner = padded.shape[3]
    outer = weights.shape[0]
    summed = jnp.zeros((frames * rows * cols, outer), jnp.float32)
    for frame_tap in range(3):
        columns = jnp.concatenate(
            [
                padded[
                    frame_tap : frame_tap + frames,
                    row_tap : row_tap + rows,
                    col_tap : col_tap + cols,
                ]
                for row_tap in range(3)
                for col_tap in range(3)
            ],
            axis=-1,
        )
        columns = columns.reshape(frames * rows * cols, 9 * inner)
        taps = weights[:, 9 * frame_tap : 9 * frame_tap + 9, :].reshape(outer, 9 * inner)
        summed = summed + lax.dot_general(
            columns, taps, (((1,), (1,)), ((), ())), preferred_element_type=jnp.float32
        )
    return summed.reshape(frames, rows, cols, outer)


def causal_layer(active, weights):
    earlier = shifted(active[-2:], "tm", 1)
    extended = jnp.concatenate([earlier, active], axis=0)
    rimmed = with_halo(extended, (("space", 1),), 1)
    padded = jnp.pad(rimmed, ((0, 0), (0, 0), (1, 1), (0, 0)))
    copies = lax.axis_size(("space", "clip"))
    share = weights.shape[2] // copies
    mine = lax.dynamic_slice_in_dim(weights, lax.axis_index(("space", "clip")) * share, share, 2)
    slices = lax.all_gather(mine, "tm", axis=0, tiled=True)
    return conv_taps(padded, lax.all_gather(slices, ("space", "clip"), axis=2, tiled=True))


def shards(
    features,
    frame_counts,
    routes,
    norm_gains,
    conv_weights,
    conv_biases,
    latent_weight,
    embed_weight,
    embed_bias,
):
    inputs = features[0].astype(jnp.float32)
    frames, rows, cols, width = inputs.shape
    active = norm_silu(inputs, norm_gains[0]).astype(jnp.bfloat16)
    hidden = causal_layer(active, conv_weights[0]) + conv_biases[0]
    active = norm_silu(hidden, norm_gains[1]).astype(jnp.bfloat16)
    hidden = causal_layer(active, conv_weights[1]) + conv_biases[1]
    merged = inputs + hidden
    active = norm_silu(merged, norm_gains[2]).astype(jnp.bfloat16)
    latent = jnp.dot(active.reshape(-1, width), latent_weight, preferred_element_type=jnp.float32)
    channels = latent_weight.shape[1]
    latent = latent.reshape(frames, rows // 2, 2, cols // 2, 2, channels)
    patches = latent.transpose(0, 1, 3, 2, 4, 5).reshape(-1, 4 * channels).astype(jnp.bfloat16)
    tok_count = patches.shape[0]
    owners = lax.axis_size("tm") * lax.axis_size("space")
    most_rows = (tok_count + owners - 1) // owners + 1
    destinations = routes[0, :, 0]
    positions = jnp.arange(tok_count, dtype=jnp.int32)
    before = positions[:, None] > positions[None, :]
    ranks = jnp.sum(
        ((destinations[:, None] == destinations[None, :]) & before).astype(jnp.int32), axis=1
    )
    targets = destinations * most_rows + ranks
    frame_ids = lax.axis_index("tm") * frames + positions // (rows // 2 * (cols // 2))
    alive = (frame_ids < frame_counts[0]).astype(jnp.bfloat16)
    placing = (jnp.arange(owners * most_rows, dtype=jnp.int32)[:, None] == targets[None, :]).astype(
        jnp.bfloat16
    )
    outgoing = jnp.dot(placing, patches, preferred_element_type=jnp.float32).astype(jnp.bfloat16)
    outgoing = outgoing.reshape(owners, most_rows, 4 * channels)
    marks = jnp.dot(placing, alive[:, None], preferred_element_type=jnp.float32).astype(
        jnp.bfloat16
    )
    marks = marks.reshape(owners, most_rows)
    tokens = lax.all_to_all(outgoing, ("tm", "space"), split_axis=0, concat_axis=0, tiled=True)
    flags = lax.all_to_all(marks, ("tm", "space"), split_axis=0, concat_axis=0, tiled=True)
    projected = (
        jnp.dot(
            tokens.reshape(-1, tokens.shape[2]), embed_weight, preferred_element_type=jnp.float32
        )
        + embed_bias
    )
    projected = projected * flags.reshape(-1, 1).astype(jnp.float32)
    packed_rows = projected.astype(jnp.bfloat16).reshape(tokens.shape[0], tokens.shape[1], -1)
    return packed_rows.reshape(1, -1, packed_rows.shape[2])


def solution(mesh):
    return jax.shard_map(
        shards,
        mesh=mesh,
        in_specs=(
            P(("groups", "clip"), "tm", "space", None, None),
            P(("groups", "clip")),
            P(("groups", "clip"), ("tm", "space"), None),
            P(),
            P(None, "tm", None, None),
            P(),
            P(),
            P(),
            P(),
        ),
        out_specs=P(("groups", "clip"), ("tm", "space"), None),
        check_vma=False,
    )
```

profile of v0, /device:TPU:0, one launch (start us, length us, event | category | flops | bytes accessed | tf_op | source)
XLA Modules:
  0.0 164.7 jit_solution(14299890801617923095)
XLA Ops:
  6.5 1.6 fusion.52
  8.6 39.7 %all-gather = bf16[1,256,27,64]{3,2,0,1:T(8,128)(2,1)S(1)} all-gather(bf16[1,64,27,64]{3,2,0,1:T(8,128)(2,1)S(1)} %copy.34), channel_id=2, replica_groups=mesh['groups'=2,'tm'=4,'space'=2,'clip'=2] {'tm'}, dimensions={1}, use_global_device_ids=true | all-gather | bytes 1105920 | tf_op jit(solution)/shard_map/all_gather | solution.py:71
  48.3 2.7 %copy.25 = bf16[1,256,27,64]{1,3,2,0:T(8,128)(2,1)} copy(bf16[1,256,27,64]{3,2,0,1:T(8,128)(2,1)S(1)} %all-gather) | data formatting | bytes 1769472 | tf_op jit(solution)/shard_map/all_gather | solution.py:71
  51.6 37.3 %all-gather.2 = bf16[1,256,27,64]{3,2,0,1:T(8,128)(2,1)S(1)} all-gather(bf16[1,64,27,64]{3,2,0,1:T(8,128)(2,1)S(1)} %copy.36), channel_id=4, replica_groups=mesh['groups'=2,'tm'=4,'space'=2,'clip'=2] {'tm'}, dimensions={1}, use_global_device_ids=true | all-gather | bytes 1105920 | tf_op jit(solution)/shard_map/all_gather | solution.py:71
  88.9 2.7 %copy.27 = bf16[1,256,27,64]{1,3,2,0:T(8,128)(2,1)} copy(bf16[1,256,27,64]{3,2,0,1:T(8,128)(2,1)S(1)} %all-gather.2) | data formatting | bytes 1769472 | tf_op jit(solution)/shard_map/all_gather | solution.py:71
  92.0 3.5 %collective-permute-start = (bf16[2,4,16,256]{3,2,1,0:T(8,128)(2,1)S(1)}, bf16[2,4,16,256]{3,2,1,0:T(8,128)(2,1)S(1)}, u32[]{:S(2)}, u32[]{:S(2)}) collective-permute-start(bf16[2,4,16,256]{3,2,1,0:T(8,128)(2,1)S(1)} %slice.322), channel_id=1, source_target_pairs={{0,4},{4,8},{8,12},{1,5},{5,9},{9,13},{2,6},{6,10},{10,14},{3,7},{... | collective-permute-start | bytes 196616 | tf_op jit(solution)/shard_map/ppermute | solution.py:10
  95.7 1.7 %collective-permute-done = bf16[2,4,16,256]{3,2,1,0:T(8,128)(2,1)S(1)} collective-permute-done((bf16[2,4,16,256]{3,2,1,0:T(8,128)(2,1)S(1)}, bf16[2,4,16,256]{3,2,1,0:T(8,128)(2,1)S(1)}, u32[]{:S(2)}, u32[]{:S(2)}) %collective-permute-start) | collective-permute-done | bytes 65568 | tf_op jit(solution)/shard_map/ppermute | solution.py:10
  97.4 3.4 %collective-permute-start.1 = (bf16[6,1,16,256]{3,2,1,0:T(8,128)(2,1)S(1)}, bf16[6,1,16,256]{3,2,1,0:T(8,128)(2,1)S(1)}, u32[]{:S(2)}, u32[]{:S(2)}) collective-permute-start(bf16[6,1,16,256]{3,2,1,0:T(8,128)(2,1)S(1)} %get-tuple-element.71), channel_id=1, source_target_pairs={{0,2},{1,3},{4,6},{5,7},{8,10},{9,11},{12,14},{13,15},{16,18},{17,... | collective-permute-start | bytes 147464 | tf_op jit(solution)/shard_map/ppermute | solution.py:21
  100.8 1.3 collective-permute-start.2
  103.3 4.6 %collective-permute-done.2 = bf16[6,1,16,256]{3,2,1,0:T(8,128)(2,1)S(1)} collective-permute-done((bf16[6,1,16,256]{3,2,1,0:T(8,128)(2,1)S(1)}, bf16[6,1,16,256]{3,2,1,0:T(8,128)(2,1)S(1)}, u32[]{:S(2)}, u32[]{:S(2)}) %collective-permute-start.2) | collective-permute-done | bytes 49184 | tf_op jit(solution)/shard_map/ppermute | solution.py:23
  108.3 0.8 slice_dynamic-update-slice_fusion.31
  109.1 0.8 slice_dynamic-update-slice_fusion.30
  109.8 0.8 slice_dynamic-update-slice_fusion.29
  110.6 0.8 slice_dynamic-update-slice_fusion.28
  111.4 0.8 fusion.27
  112.2 0.8 slice_dynamic-update-slice_fusion.27
  113.1 0.8 slice_dynamic-update-slice_fusion.26
  113.8 0.8 slice_dynamic-update-slice_fusion.25
  114.6 0.8 slice_dynamic-update-slice_fusion.24
  115.4 2.2 %fusion.51 = (bf16[256,9,256]{0,2,1:T(8,128)(2,1)S(1)}, bf16[256,9,256]{0,2,1:T(8,128)(2,1)S(1)}, bf16[256,9,256]{0,2,1:T(8,128)(2,1)S(1)}) fusion(bf16[256,27,256]{0,2,1:T(8,128)(2,1)} %bitcast.85), kind=kLoop, calls=%fused_computation.153 | loop fusion | bytes 7077888 | tf_op jit(solution)/shard_map/slice | solution.py:56
  117.6 1.7 %fusion.56 = f32[256,256]{1,0:T(8,128)S(1)} fusion(bf16[256,2304]{1,0:T(8,128)(2,1)} %bitcast.4, bf16[256,2304]{0,1:T(8,128)(2,1)S(1)} %bitcast.83), kind=kOutput, calls=%fused_computation.158 | convolution fusion | flops 301989888 | bytes 2621440 | tf_op jit(solution)/shard_map/dot_general | solution.py:57
  119.4 1.8 %convolution_add_fusion.4 = f32[256,256]{1,0:T(8,128)S(1)} fusion(f32[256,256]{1,0:T(8,128)S(1)} %fusion.56, bf16[256,2304]{1,0:T(8,128)(2,1)} %bitcast.7, bf16[256,2304]{0,1:T(8,128)(2,1)S(1)} %bitcast.82), kind=kOutput, calls=%fused_computation.9 | convolution fusion | flops 302055424 | bytes 2883584 | tf_op jit(solution)/shard_map/dot_general | solution.py:57
  122.0 4.3 %collective-permute-start.3 = (bf16[2,4,16,256]{3,2,1,0:T(8,128)(2,1)S(1)}, bf16[2,4,16,256]{3,2,1,0:T(8,128)(2,1)S(1)}, u32[]{:S(2)}, u32[]{:S(2)}) collective-permute-start(bf16[2,4,16,256]{3,2,1,0:T(8,128)(2,1)S(1)} %slice.356), channel_id=1, source_target_pairs={{0,4},{4,8},{8,12},{1,5},{5,9},{9,13},{2,6},{6,10},{10,14},{3,7},{... | collective-permute-start | bytes 196616 | tf_op jit(solution)/shard_map/ppermute | solution.py:10
  127.1 4.4 %all-to-all-start.1 = ((bf16[8,1,9]{2,1,0:T(2,128)(2,1)}), bf16[8,1,9]{2,1,0:T(2,128)(2,1)S(1)}, u32[]{:S(2)}, u32[]{:S(2)}) async-start(bf16[8,1,9]{2,1,0:T(2,128)(2,1)} %all_to_all.12), calls=%async_computation.1 | async-start | bytes 8192 | tf_op jit(solution)/shard_map/all_to_all | solution.py:120
  131.5 3.9 %collective-permute-start.4 = (bf16[6,1,16,256]{3,2,1,0:T(8,128)(2,1)S(1)}, bf16[6,1,16,256]{3,2,1,0:T(8,128)(2,1)S(1)}, u32[]{:S(2)}, u32[]{:S(2)}) collective-permute-start(bf16[6,1,16,256]{3,2,1,0:T(8,128)(2,1)S(1)} %get-tuple-element.65), channel_id=1, source_target_pairs={{0,2},{1,3},{4,6},{5,7},{8,10},{9,11},{12,14},{13,15},{16,18},{17,... | collective-permute-start | bytes 147464 | tf_op jit(solution)/shard_map/ppermute | solution.py:21
  135.4 1.3 collective-permute-start.5
  136.7 2.2 %fusion.50 = (bf16[256,9,256]{0,2,1:T(8,128)(2,1)S(1)}, bf16[256,9,256]{0,2,1:T(8,128)(2,1)S(1)}, bf16[256,9,256]{0,2,1:T(8,128)(2,1)S(1)}) fusion(bf16[256,27,256]{0,2,1:T(8,128)(2,1)} %bitcast.84), kind=kLoop, calls=%fused_computation.152 | loop fusion | bytes 7077888 | tf_op jit(solution)/shard_map/slice | solution.py:56
  139.0 2.4 %collective-permute-done.5 = bf16[6,1,16,256]{3,2,1,0:T(8,128)(2,1)S(1)} collective-permute-done((bf16[6,1,16,256]{3,2,1,0:T(8,128)(2,1)S(1)}, bf16[6,1,16,256]{3,2,1,0:T(8,128)(2,1)S(1)}, u32[]{:S(2)}, u32[]{:S(2)}) %collective-permute-start.5) | collective-permute-done | bytes 49184 | tf_op jit(solution)/shard_map/ppermute | solution.py:23
  144.9 0.7 reshape.170
  145.6 4.5 %all-to-all-start = ((bf16[8,2,288]{2,1,0:T(2,128)(2,1)}), bf16[8,2,288]{2,1,0:T(2,128)(2,1)S(1)}, u32[]{:S(2)}, u32[]{:S(2)}) async-start(bf16[8,2,288]{2,1,0:T(2,128)(2,1)} %reshape.170), calls=%async_computation | async-start | bytes 24576 | tf_op jit(solution)/shard_map/all_to_all | solution.py:119
  150.3 6.4 %all-to-all-done = bf16[8,2,288]{2,1,0:T(2,128)(2,1)S(1)} async-done(((bf16[8,2,288]{2,1,0:T(2,128)(2,1)}), bf16[8,2,288]{2,1,0:T(2,128)(2,1)S(1)}, u32[]{:S(2)}, u32[]{:S(2)}) %all-to-all-start) | async-done | bytes 9248 | tf_op jit(solution)/shard_map/all_to_all | solution.py:119
  156.9 1.0 fusion.2
  (76 shorter events, 7.7 us)
Async XLA Ops:
  6.5 150.3 %copy-start = (bf16[64,3072]{1,0:T(8,128)(2,1)S(1)}, bf16[64,3072]{1,0:T(8,128)(2,1)}, u32[]{:S(2)}) copy-start(bf16[64,3072]{1,0:T(8,128)(2,1)} %param.16) | copy-start | bytes 1179652
  6.5 108.9 %all-gather.7.cloned.1.call-start = ((), (), s32[]{:S(2)}) async-start(), calls=%async_computation.2 | async-start | bytes 4423680 | tf_op jit(solution)/shard_map/all_gather | solution.py:72
  51.1 85.7 %all-gather.9.cloned.1.call-start = ((), (), s32[]{:S(2)}) async-start(), calls=%async_computation.3 | async-start | bytes 4423680 | tf_op jit(solution)/shard_map/all_gather | solution.py:72
  88.9 2.7 %copy-start.1 = (bf16[1,4,4,16,256]{4,3,2,1,0:T(8,128)(2,1)S(1)}, bf16[1,4,4,16,256]{4,3,2,1,0:T(8,128)(2,1)}, u32[]{:S(2)}) copy-start(bf16[1,4,4,16,256]{4,3,2,1,0:T(8,128)(2,1)} %param.9) | copy-start | bytes 393220
  88.9 2.9 %copy-start.4 = (f32[3,256]{1,0:T(4,128)S(1)}, f32[3,256]{1,0:T(4,128)}, u32[]{:S(2)}) copy-start(f32[3,256]{1,0:T(4,128)} %param.12) | copy-start | bytes 9220
  91.6 3.9 %copy-start.5 = (f32[2,256]{1,0:T(2,128)S(1)}, f32[2,256]{1,0:T(2,128)}, u32[]{:S(2)}) copy-start(f32[2,256]{1,0:T(2,128)} %param.14) | copy-start | bytes 6148
  91.6 3.9 %copy-start.6 = (s32[1,64,1]{1,2,0:T(1,128)S(1)}, s32[1,64,1]{1,2,0:T(1,128)}, u32[]{:S(2)}) copy-start(s32[1,64,1]{1,2,0:T(1,128)} %param.11) | copy-start | bytes 772
  92.0 5.4 %collective-permute-start = (bf16[2,4,16,256]{3,2,1,0:T(8,128)(2,1)S(1)}, bf16[2,4,16,256]{3,2,1,0:T(8,128)(2,1)S(1)}, u32[]{:S(2)}, u32[]{:S(2)}) collective-permute-start(bf16[2,4,16,256]{3,2,1,0:T(8,128)(2,1)S(1)} %slice.322), channel_id=1, source_target_pairs={{0,4},{4,8},{8,12},{1,5},{5,9},{9,13},{2,6},{6,10},{10,14},{3,7},{... | collective-permute-start | bytes 196616 | tf_op jit(solution)/shard_map/ppermute | solution.py:10
  97.4 5.9 %collective-permute-start.1 = (bf16[6,1,16,256]{3,2,1,0:T(8,128)(2,1)S(1)}, bf16[6,1,16,256]{3,2,1,0:T(8,128)(2,1)S(1)}, u32[]{:S(2)}, u32[]{:S(2)}) collective-permute-start(bf16[6,1,16,256]{3,2,1,0:T(8,128)(2,1)S(1)} %get-tuple-element.71), channel_id=1, source_target_pairs={{0,2},{1,3},{4,6},{5,7},{8,10},{9,11},{12,14},{13,15},{16,18},{17,... | collective-permute-start | bytes 147464 | tf_op jit(solution)/shard_map/ppermute | solution.py:21
  100.8 7.2 %collective-permute-start.2 = (bf16[6,1,16,256]{3,2,1,0:T(8,128)(2,1)S(1)}, bf16[6,1,16,256]{3,2,1,0:T(8,128)(2,1)S(1)}, u32[]{:S(2)}, u32[]{:S(2)}) collective-permute-start(bf16[6,1,16,256]{3,2,1,0:T(8,128)(2,1)S(1)} %get-tuple-element.72), channel_id=1, source_target_pairs={{2,0},{3,1},{6,4},{7,5},{10,8},{11,9},{14,12},{15,13},{18,16},{19,... | collective-permute-start | bytes 147464 | tf_op jit(solution)/shard_map/ppermute | solution.py:23
  122.0 9.5 %collective-permute-start.3 = (bf16[2,4,16,256]{3,2,1,0:T(8,128)(2,1)S(1)}, bf16[2,4,16,256]{3,2,1,0:T(8,128)(2,1)S(1)}, u32[]{:S(2)}, u32[]{:S(2)}) collective-permute-start(bf16[2,4,16,256]{3,2,1,0:T(8,128)(2,1)S(1)} %slice.356), channel_id=1, source_target_pairs={{0,4},{4,8},{8,12},{1,5},{5,9},{9,13},{2,6},{6,10},{10,14},{3,7},{... | collective-permute-start | bytes 196616 | tf_op jit(solution)/shard_map/ppermute | solution.py:10
  127.1 18.6 %all-to-all-start.1 = ((bf16[8,1,9]{2,1,0:T(2,128)(2,1)}), bf16[8,1,9]{2,1,0:T(2,128)(2,1)S(1)}, u32[]{:S(2)}, u32[]{:S(2)}) async-start(bf16[8,1,9]{2,1,0:T(2,128)(2,1)} %all_to_all.12), calls=%async_computation.1 | async-start | bytes 8192 | tf_op jit(solution)/shard_map/all_to_all | solution.py:120
  131.5 7.5 %collective-permute-start.4 = (bf16[6,1,16,256]{3,2,1,0:T(8,128)(2,1)S(1)}, bf16[6,1,16,256]{3,2,1,0:T(8,128)(2,1)S(1)}, u32[]{:S(2)}, u32[]{:S(2)}) collective-permute-start(bf16[6,1,16,256]{3,2,1,0:T(8,128)(2,1)S(1)} %get-tuple-element.65), channel_id=1, source_target_pairs={{0,2},{1,3},{4,6},{5,7},{8,10},{9,11},{12,14},{13,15},{16,18},{17,... | collective-permute-start | bytes 147464 | tf_op jit(solution)/shard_map/ppermute | solution.py:21
  135.4 6.0 %collective-permute-start.5 = (bf16[6,1,16,256]{3,2,1,0:T(8,128)(2,1)S(1)}, bf16[6,1,16,256]{3,2,1,0:T(8,128)(2,1)S(1)}, u32[]{:S(2)}, u32[]{:S(2)}) collective-permute-start(bf16[6,1,16,256]{3,2,1,0:T(8,128)(2,1)S(1)} %get-tuple-element.66), channel_id=1, source_target_pairs={{2,0},{3,1},{6,4},{7,5},{10,8},{11,9},{14,12},{15,13},{18,16},{19,... | collective-permute-start | bytes 147464 | tf_op jit(solution)/shard_map/ppermute | solution.py:23
  143.6 0.7 copy-start.3
  143.6 13.3 %copy-start.2 = (f32[3072]{0:T(1024)S(1)}, f32[3072]{0:T(1024)}, u32[]{:S(2)}) copy-start(f32[3072]{0:T(1024)} %param.17) | copy-start | bytes 36868
  145.6 11.1 %all-to-all-start = ((bf16[8,2,288]{2,1,0:T(2,128)(2,1)}), bf16[8,2,288]{2,1,0:T(2,128)(2,1)S(1)}, u32[]{:S(2)}, u32[]{:S(2)}) async-start(bf16[8,2,288]{2,1,0:T(2,128)(2,1)} %reshape.170), calls=%async_computation | async-start | bytes 24576 | tf_op jit(solution)/shard_map/all_to_all | solution.py:119
Sparse Core Ops, SparseCore 0:
  51.2 32.3 all-gather.6
  91.8 33.0 all-gather.8
where the time goes:
time: 165 us
  blocking collectives  77 us (47%)
  starting transfers between devices  26.6 us (16%)
  local copies, waits for them, and re-layouts  21.5 us (13%)
  waiting for transfers between devices  15.8 us (10%)
  between operations  14.5 us (9%)
  matrix products  7 us (4%)
  other arithmetic  2.28 us (1%)
    all_gather x2, blocking collectives, causal_layer(): slices = lax.all_gather(mine, 'tm', axis=0, tiled=True)  77 us
    ppermute x2, starting transfers between devices, shifted(): return lax.ppermute(block, axis, route)  7.8 us
    unnamed x32, local copies, waits for them, and re-layouts  7.52 us
    ppermute x2, starting transfers between devices, with_halo(): lax.ppermute(tail, axis, [(i, (i + 1) % count) for i in range(ends)])  7.32 us
    ppermute x2, waiting for transfers between devices, with_halo(): lax.ppermute(head, axis, [((i + 1) % count, i) for i in range(ends)])  7.07 us
    all_to_all x1, waiting for transfers between devices, shards(): lax.all_to_all(outgoing, ('tm', 'space'), split_axis=0, concat_axis=0, ti...  6.45 us
    dot_general x6, matrix products, conv_taps(): lax.dot_general(columns, taps, (((1,), (1,)), ((), ())), preferred_elemen...  5.49 us
    all_gather x2, local copies, waits for them, and re-layouts, causal_layer(): slices = lax.all_gather(mine, 'tm', axis=0, tiled=True)  5.42 us
  transfers between devices with their start and end apart: 10, of which 5 were waited for; matrix products, arithmetic and copies ran while one was open for 15% of the time, Pallas kernels for 0%

commit v1 on v0

v1 whole, which is shorter than its diff:
```python
import functools

import jax
import jax.numpy as jnp
from jax import lax
from jax.experimental import pallas as pl
from jax.experimental.pallas import tpu as pltpu
from jax.sharding import PartitionSpec as P

MESH = pl.DeviceIdType.MESH
LANES = 128
SUBLANES = 16


def norm_silu(values, gain):
    scale = lax.rsqrt(jnp.mean(values * values, axis=-1, keepdims=True) + 1e-06)
    scaled = values * scale * gain
    return scaled / (1.0 + jnp.exp(-scaled))


def encoder(
    n, ns, most, width_latent,
    feat, weights_any, gains, biases, latent_wide, targets, count,
    tokens_out,
    first, second, raw, taps, slab_out, slab_in, tok_out, tok_in,
    raw_sem, block_send, block_recv, up_send, up_recv, down_send, down_recv,
    slab_send, slab_recv, tok_send, tok_recv,
):
    t = lax.axis_index("tm")
    s = lax.axis_index("space")
    me = t * ns + s
    owners = n * ns
    frames, rows, cols, width = feat.shape
    cells = frames * rows * cols
    out = weights_any.shape[1]
    pack = max(1, LANES // out)
    part = cells // pack
    step = jnp.where(t < n // 2, 1, -1)

    barrier = pltpu.get_barrier_semaphore()

    def greet(d, carry):
        o = (me + d) % owners
        pl.semaphore_signal(
            barrier, inc=1, device_id={"tm": o // ns, "space": o % ns}, device_id_type=MESH
        )
        return carry

    lax.fori_loop(1, owners, greet, 0)
    weight_copy = pltpu.make_async_copy(weights_any, raw, raw_sem)
    weight_copy.start()

    for buf in (first, second):
        buf[0:2] = jnp.zeros((2,) + buf.shape[1:], buf.dtype)

        @pl.when(s == 0)
        def _():
            buf[:, 0:1] = jnp.zeros((buf.shape[0], 1) + buf.shape[2:], buf.dtype)

        @pl.when(s == ns - 1)
        def _():
            buf[:, rows + 1 : rows + 2] = jnp.zeros((buf.shape[0], 1) + buf.shape[2:], buf.dtype)

    inputs = feat[...].reshape(cells, width).astype(jnp.float32)

    def keep(buf, active):
        buf[pl.ds(2 + frames * t, frames), 1 : rows + 1] = active.astype(jnp.bfloat16).reshape(
            frames, rows, cols, width
        )

    def block_copy(buf, layer, source, target):
        span = buf.at[pl.ds(2 + frames * source, frames), pl.ds(1, rows)]
        return pltpu.make_async_remote_copy(
            src_ref=span, dst_ref=span,
            send_sem=block_send.at[layer, target], recv_sem=block_recv.at[layer, source],
            device_id={"tm": target}, device_id_type=MESH,
        )

    def up_copy(buf, layer, source, target, side):
        return pltpu.make_async_remote_copy(
            src_ref=buf.at[pl.ds(2 + frames * source, frames), pl.ds(1, 1)],
            dst_ref=buf.at[pl.ds(2 + frames * source, frames), pl.ds(rows + 1, 1)],
            send_sem=up_send.at[layer, target], recv_sem=up_recv.at[layer, source],
            device_id={"tm": target, "space": side}, device_id_type=MESH,
        )

    def down_copy(buf, layer, source, target, side):
        return pltpu.make_async_remote_copy(
            src_ref=buf.at[pl.ds(2 + frames * source, frames), pl.ds(rows, 1)],
            dst_ref=buf.at[pl.ds(2 + frames * source, frames), pl.ds(0, 1)],
            send_sem=down_send.at[layer, target], recv_sem=down_recv.at[layer, source],
            device_id={"tm": target, "space": side}, device_id_type=MESH,
        )

    def slab_copy(layer, source, target):
        return pltpu.make_async_remote_copy(
            src_ref=slab_out.at[layer, target], dst_ref=slab_in.at[layer, source],
            send_sem=slab_send.at[layer, target], recv_sem=slab_recv.at[layer, source],
            device_id={"tm": target}, device_id_type=MESH,
        )

    def spread(buf, layer):
        def send(k, carry):
            target = (t + k * step + n) % n

            @pl.when(k > 0)
            def _():
                block_copy(buf, layer, t, target).start()

            @pl.when(s > 0)
            def _():
                up_copy(buf, layer, t, target, s - 1).start()

            @pl.when(s < ns - 1)
            def _():
                down_copy(buf, layer, t, target, s + 1).start()

            return carry

        lax.fori_loop(0, n, send, 0)

    def spread_sent(buf, layer):
        def sent(k, carry):
            target = (t + k * step + n) % n

            @pl.when(k > 0)
            def _():
                block_copy(buf, layer, t, target).wait_send()
                slab_copy(layer, t, target).wait_send()

            @pl.when(s > 0)
            def _():
                up_copy(buf, layer, t, target, s - 1).wait_send()

            @pl.when(s < ns - 1)
            def _():
                down_copy(buf, layer, t, target, s + 1).wait_send()

            return carry

        lax.fori_loop(0, n, sent, 0)

    def arrive(buf, layer, c):
        @pl.when(c != t)
        def _():
            block_copy(buf, layer, c, c).wait_recv()

        @pl.when(s < ns - 1)
        def _():
            up_copy(buf, layer, c, c, s + 1).wait_recv()

        @pl.when(s > 0)
        def _():
            down_copy(buf, layer, c, c, s - 1).wait_recv()

    column = lax.broadcasted_iota(jnp.int32, (cells, 1), 0) % cols

    def convolve(buf, layer):
        def place(b):
            return ((b - t) * step + n) % n

        def one(k, carry):
            b = (t + k * step + n) % n
            here = place(b)

            @pl.when((b == n - 1) | (place((b + 1) % n) > here))
            def _():
                arrive(buf, layer, b)

            @pl.when((b > 0) & (place((b + n - 1) % n) > here))
            def _():
                arrive(buf, layer, (b + n - 1) % n)

            total = jnp.zeros((cells, 3 * out), jnp.float32)
            for a in range(3):
                for r in range(3):
                    block = buf[pl.ds(frames * b + a, frames), r : r + rows]
                    total = total + lax.dot_general(
                        block.reshape(cells, width), taps[layer, 3 * a + r],
                        (((1,), (1,)), ((), ())), preferred_element_type=jnp.float32,
                    )
            left = jnp.where(column == 0, 0.0, pltpu.roll(total[:, :out], 1, 0))
            right = jnp.where(column == cols - 1, 0.0, pltpu.roll(total[:, 2 * out :], cells - 1, 0))
            summed = (left + total[:, out : 2 * out] + right).astype(jnp.bfloat16)
            packed = jnp.concatenate(
                [summed[j * part : (j + 1) * part] for j in range(pack)], axis=1
            )

            @pl.when(b == t)
            def _():
                slab_in[layer, pl.ds(t, 1)] = packed[None]

            @pl.when(b != t)
            def _():
                slab_out[layer, pl.ds(b, 1)] = packed[None]
                slab_copy(layer, t, b).start()

            return carry

        lax.fori_loop(0, n, one, 0)

        def came(k, carry):
            slab_copy(layer, (t + k) % n, (t + k) % n).wait_recv()
            return carry

        lax.fori_loop(1, n, came, 0)
        pieces = [slab_in[layer, q].astype(jnp.float32) for q in range(n)]
        hidden = jnp.concatenate(
            [
                jnp.concatenate([piece[:, j * out : (j + 1) * out] for piece in pieces], axis=1)
                for j in range(pack)
            ],
            axis=0,
        )
        return hidden + biases[layer : layer + 1]

    keep(first, norm_silu(inputs, gains[0:1]))
    pl.semaphore_wait(barrier, owners - 1)
    spread(first, 0)
    weight_copy.wait()
    for layer in range(2):
        for tap in range(27):
            group, e = tap // 3, tap % 3
            taps[layer, group, e * out : (e + 1) * out] = raw[layer, :, tap, :]
    hidden = convolve(first, 0)
    keep(second, norm_silu(hidden, gains[1:2]))
    spread(second, 1)
    hidden = convolve(second, 1)
    merged = feat[...].reshape(cells, width).astype(jnp.float32) + hidden
    active = norm_silu(merged, gains[2:3]).astype(jnp.bfloat16)
    latent = jnp.dot(active, latent_wide[...], preferred_element_type=jnp.float32)
    cell = lax.broadcasted_iota(jnp.int32, (cells, LANES), 0)
    lane = lax.broadcasted_iota(jnp.int32, (cells, LANES), 1)
    corner = (cell // cols % 2) * 2 + cell % 2
    alive = (t * frames + cell // (rows * cols) < count[0]) & (corner == 0)
    flagged = jnp.where((lane == 4 * width_latent) & alive, 1.0, 0.0)
    patches = jnp.where(lane // width_latent == corner, latent, flagged).astype(jnp.bfloat16)
    slots = lax.broadcasted_iota(jnp.int32, (owners * SUBLANES, cells), 0)
    placing = jnp.where(slots == targets[...], 1.0, 0.0).astype(jnp.bfloat16)
    outgoing = jnp.dot(placing, patches, preferred_element_type=jnp.float32).astype(jnp.bfloat16)
    tok_out[...] = outgoing.reshape(owners, SUBLANES, LANES)
    tok_in[pl.ds(me, 1)] = tok_out[pl.ds(me, 1)]

    def tok_copy(source, target):
        return pltpu.make_async_remote_copy(
            src_ref=tok_out.at[target], dst_ref=tok_in.at[source],
            send_sem=tok_send.at[target], recv_sem=tok_recv.at[source],
            device_id={"tm": target // ns, "space": target % ns}, device_id_type=MESH,
        )

    def tok_start(d, carry):
        tok_copy(me, (me + d) % owners).start()
        return carry

    def tok_wait(d, carry):
        o = (me + d) % owners
        tok_copy(o, o).wait_recv()
        return carry

    def tok_sent(d, carry):
        tok_copy(me, (me + d) % owners).wait_send()
        return carry

    lax.fori_loop(1, owners, tok_start, 0)
    spread_sent(first, 0)
    spread_sent(second, 1)
    lax.fori_loop(1, owners, tok_wait, 0)
    row = lax.broadcasted_iota(jnp.int32, (owners * most, owners * SUBLANES), 0)
    held = lax.broadcasted_iota(jnp.int32, (owners * most, owners * SUBLANES), 1)
    inner = held % SUBLANES
    chosen = (row == held // SUBLANES * most + inner) & (inner < most)
    tokens_out[...] = jnp.dot(
        jnp.where(chosen, 1.0, 0.0).astype(jnp.bfloat16),
        tok_in[...].reshape(owners * SUBLANES, LANES),
        preferred_element_type=jnp.float32,
    ).astype(jnp.bfloat16)
    lax.fori_loop(1, owners, tok_sent, 0)


def shards(
    features,
    frame_counts,
    routes,
    norm_gains,
    conv_weights,
    conv_biases,
    latent_weight,
    embed_weight,
    embed_bias,
):
    feat = features[0]
    frames, rows, cols, width = feat.shape
    cells = frames * rows * cols
    n, ns = lax.axis_size("tm"), lax.axis_size("space")
    owners = n * ns
    out = conv_weights.shape[1]
    pack = max(1, LANES // out)
    latents = latent_weight.shape[1]
    tok_count = routes.shape[1]
    most = (tok_count + owners - 1) // owners + 1
    destinations = routes[0, :, 0]
    positions = jnp.arange(tok_count, dtype=jnp.int32)
    before = positions[:, None] > positions[None, :]
    ranks = jnp.sum(
        ((destinations[:, None] == destinations[None, :]) & before).astype(jnp.int32), axis=1
    )
    slots = (destinations * SUBLANES + ranks).reshape(frames, rows // 2, 1, cols // 2, 1)
    targets = jnp.broadcast_to(slots, (frames, rows // 2, 2, cols // 2, 2)).reshape(1, cells)
    latent_wide = jnp.pad(
        jnp.concatenate([latent_weight] * 4, axis=1), ((0, 0), (0, LANES - 4 * latents))
    )
    vmem = pl.BlockSpec(memory_space=pltpu.VMEM)
    dma = pltpu.SemaphoreType.DMA
    field = pltpu.VMEM((n * frames + 2, rows + 2, cols, width), jnp.bfloat16)
    slab = pltpu.VMEM((2, n, cells // pack, pack * out), jnp.bfloat16)
    tok = pltpu.VMEM((owners, SUBLANES, LANES), jnp.bfloat16)
    tokens = pl.pallas_call(
        functools.partial(encoder, n, ns, most, latents),
        out_shape=jax.ShapeDtypeStruct((owners * most, LANES), jnp.bfloat16),
        in_specs=[vmem, pl.BlockSpec(memory_space=pl.ANY), vmem, vmem, vmem, vmem,
                  pl.BlockSpec(memory_space=pltpu.SMEM)],
        out_specs=vmem,
        scratch_shapes=[
            field, field,
            pltpu.VMEM(conv_weights.shape, jnp.bfloat16),
            pltpu.VMEM((2, 9, 3 * out, width), jnp.bfloat16),
            slab, slab, tok, tok,
            dma,
            dma((2, n)), dma((2, n)), dma((2, n)), dma((2, n)), dma((2, n)), dma((2, n)),
            dma((2, n)), dma((2, n)), dma((owners,)), dma((owners,)),
        ],
        compiler_params=pltpu.CompilerParams(collective_id=0, has_side_effects=True),
    )(feat, conv_weights, norm_gains, conv_biases, latent_wide, targets, frame_counts)
    channels = 4 * latents
    projected = (
        jnp.dot(tokens[:, :channels], embed_weight, preferred_element_type=jnp.float32) + embed_bias
    ) * tokens[:, channels : channels + 1].astype(jnp.float32)
    return projected.astype(jnp.bfloat16)[None]


def solution(mesh):
    return jax.shard_map(
        shards,
        mesh=mesh,
        in_specs=(
            P(("groups", "clip"), "tm", "space", None, None),
            P(("groups", "clip")),
            P(("groups", "clip"), ("tm", "space"), None),
            P(),
            P(None, "tm", None, None),
            P(),
            P(),
            P(),
            P(),
        ),
        out_specs=P(("groups", "clip"), ("tm", "space"), None),
        check_vma=False,
    )
```

time: 165 us -> 66.4 us (0.40)
  blocking collectives: 77 us -> 0 us
  Pallas kernels: 0 us -> 54.6 us
  starting transfers between devices: 26.6 us -> 0 us
  local copies, waits for them, and re-layouts: 21.5 us -> 5.67 us
  waiting for transfers between devices: 15.8 us -> 0 us
  between operations: 14.5 us -> 0.75 us
  matrix products: 7 us -> 1.76 us
    all_gather x2 -> x0, blocking collectives: 77 us -> none  [causal_layer(): slices = lax.all_gather(mine, 'tm', axis=0, tiled=True)]
    pallas_call x0 -> x1, Pallas kernels: none -> 54.6 us  [shards(): pl.pallas_call(functools.partial(encoder, n, ns, most, latents), out_shap...]
    ppermute x6 -> x0, starting transfers between devices: 17.7 us -> none  [the longest x2 7.8 us: shifted(): return lax.ppermute(block, axis, route)]
    ppermute x6 -> x0, waiting for transfers between devices: 9.31 us -> none  [the longest x2 7.07 us: with_halo(): lax.ppermute(head, axis, [((i + 1) % count, i) for i in range(ends)])]
    all_to_all x2 -> x0, starting transfers between devices: 8.9 us -> none  [the longest x1 4.54 us: shards(): lax.all_to_all(outgoing, ('tm', 'space'), split_axis=0, concat_axis=0, ti...]
    all_to_all x2 -> x0, waiting for transfers between devices: 6.45 us -> none  [the longest x1 6.45 us: shards(): lax.all_to_all(outgoing, ('tm', 'space'), split_axis=0, concat_axis=0, ti...]
    slice x7 -> x0, local copies, waits for them, and re-layouts: 6.04 us -> none  [the longest x2 4.42 us: conv_taps(): weights[:, 9 * frame_tap:9 * frame_tap + 9, :].reshape(outer, 9 * inner)]
    all_gather x2 -> x0, local copies, waits for them, and re-layouts: 5.42 us -> none  [causal_layer(): slices = lax.all_gather(mine, 'tm', axis=0, tiled=True)]
  transfers between devices with their start and end apart: 10 -> 0, of which waited for: 5 -> 0; matrix products, arithmetic and copies ran while one was open for 15% -> 0% of each run, Pallas kernels for 0% -> 0%
where the time goes in v1:
time: 66.4 us; the launch traced here: 66 us
  Pallas kernels  54.6 us (82%)
  local copies, waits for them, and re-layouts  5.67 us (9%)
  other arithmetic  3.25 us (5%)
  matrix products  1.76 us (3%)
  between operations  0.75 us (1%)
    pallas_call x1, Pallas kernels, shards(): pl.pallas_call(functools.partial(encoder, n, ns, most, latents), out_shap...  54.6 us
    unnamed x6, local copies, waits for them, and re-layouts  4.68 us
    dot_general x1, matrix products, shards(): jnp.dot(tokens[:, :channels], embed_weight, preferred_element_type=jnp.fl...  1.76 us

profile of v1, /device:TPU:0, one launch (start us, length us, event | category | flops | bytes accessed | tf_op | source)
XLA Modules:
  0.0 66.0 jit_solution(13891091810478918729)
XLA Ops:
  0.0 0.0 copy-start
  0.7 0.9 %convert_reduce_fusion.1 = s32[64]{0:T(128)S(1)} fusion(s32[64]{0:T(128)} %bitcast.8), kind=kLoop, calls=%fused_computation.13 | loop fusion | flops 20416 | bytes 512 | tf_op jit(solution)/shard_map/reduce_sum | solution.py:304
  1.6 0.7 %multiply_reduce_fusion = s32[64]{0:T(128)S(1)} fusion(s32[1,64,1]{1,2,0:T(1,128)} %param.11), kind=kLoop, calls=%fused_computation.17 | loop fusion | flops 64 | bytes 512 | tf_op jit(solution)/shard_map/mul | solution.py:307
  2.3 0.1 mul.28
  2.4 0.1 reduce_sum.12
  2.5 0.1 broadcast_in_dim.4
  2.6 0.7 %reshape.19.targets = s32[1,256]{1,0:T(1,128)} reshape(s32[4,2,2,8,2]{4,3,2,1,0:T(8,128)S(1)} %broadcast_in_dim.4) | data formatting | bytes 2048 | tf_op jit(solution)/shard_map/reshape | solution.py:308
  3.3 0.8 %copy.20 = bf16[256,16]{1,0:T(8,128)(2,1)S(1)} copy(bf16[256,16]{0,1:T(8,128)(2,1)} %param.15) | data formatting | bytes 16384 | tf_op args[6]
  4.1 0.8 %fusion.9.latent_wide = bf16[256,128]{1,0:T(8,128)(2,1)} fusion(bf16[256,16]{1,0:T(8,128)(2,1)S(1)} %copy.20), kind=kLoop, calls=%fused_computation.11 | loop fusion | flops 425984 | bytes 73728 | tf_op jit(solution)/shard_map/concatenate | solution.py:310
  4.9 3.9 %copy.24.weights_any = bf16[2,64,27,256]{3,2,1,0:T(8,128)(2,1)} copy(bf16[2,64,27,256]{3,1,2,0:T(8,128)(2,1)} %param.13) | data formatting | bytes 3538944 | tf_op args[4]
  8.7 0.0 copy-start.1
  8.7 54.6 %shard_map.91 = bf16[72,128]{1,0:T(8,128)(2,1)} custom-call(bf16[4,4,16,256]{3,2,1,0:T(8,128)(2,1)} %bitcast.7, bf16[2,64,27,256]{3,2,1,0:T(8,128)(2,1)} %copy.24.weights_any, f32[3,256]{1,0:T(4,128)} %gains.1, f32[2,256]{1,0:T(2,128)} %biases.1, bf16[256,128]{1,0:T(8,128)(2,1)} %fusion.9.latent_wide, s32[1,256]{1,0:T(1,128)} %reshape.19.targets, ...), custom_call_target="tpu_custom_call" | custom-call | tf_op jit(solution)/shard_map/pallas_call | solution.py:317
  63.3 0.9 %convert_reduce_fusion = f32[72]{0:T(128)S(1)} fusion(bf16[72,128]{1,0:T(8,128)(2,1)} %shard_map.91), kind=kLoop, calls=%fused_computation.12 | loop fusion | flops 72 | bytes 432 | tf_op jit(solution)/shard_map/mul | solution.py:335
  64.3 0.0 copy-done
  64.3 0.0 copy-done.1
  64.3 1.8 %fusion.2 = bf16[1,72,3072]{2,1,0:T(8,128)(2,1)} fusion(bf16[64,3072]{1,0:T(8,128)(2,1)S(1)} %copy-done, f32[72]{0:T(128)S(1)} %convert_reduce_fusion, f32[3072]{0:T(1024)S(1)} %copy-done.1, bf16[72,128]{1,0:T(8,128)(2,1)} %shard_map.91), kind=kOutput, calls=%fused_computation.3 | convolution fusion | flops 28975104 | bytes 866592 | tf_op jit(solution)/shard_map/dot_general | solution.py:336
  (1 shorter events, 0.0 us)
Async XLA Ops:
  0.0 64.3 %copy-start = (bf16[64,3072]{1,0:T(8,128)(2,1)S(1)}, bf16[64,3072]{1,0:T(8,128)(2,1)}, u32[]{:S(2)}) copy-start(bf16[64,3072]{1,0:T(8,128)(2,1)} %param.16) | copy-start | bytes 1179652
  8.7 55.5 %copy-start.1 = (f32[3072]{0:T(1024)S(1)}, f32[3072]{0:T(1024)}, u32[]{:S(2)}) copy-start(f32[3072]{0:T(1024)} %param.17) | copy-start | bytes 36868

commit v2 on v1

--- a/solution.py
+++ b/solution.py
@@ -20,9 +20,9 @@
 
 def encoder(
     n, ns, most, width_latent,
-    feat, weights_any, gains, biases, latent_wide, targets, count,
+    feat, weights_any, gains, biases, latent_rows, owner_of, count,
     tokens_out,
-    first, second, raw, taps, slab_out, slab_in, tok_out, tok_in,
+    first, second, taps, placing, slab_out, slab_in, tok_out, tok_in,
     raw_sem, block_send, block_recv, up_send, up_recv, down_send, down_recv,
     slab_send, slab_recv, tok_send, tok_recv,
 ):
@@ -32,7 +32,7 @@
     owners = n * ns
     frames, rows, cols, width = feat.shape
     cells = frames * rows * cols
-    out = weights_any.shape[1]
+    out = weights_any.shape[2] // 3
     pack = max(1, LANES // out)
     part = cells // pack
     step = jnp.where(t < n // 2, 1, -1)
@@ -47,7 +47,7 @@
         return carry
 
     lax.fori_loop(1, owners, greet, 0)
-    weight_copy = pltpu.make_async_copy(weights_any, raw, raw_sem)
+    weight_copy = pltpu.make_async_copy(weights_any, taps, raw_sem)
     weight_copy.start()
 
     for buf in (first, second):
@@ -217,27 +217,42 @@
     keep(first, norm_silu(inputs, gains[0:1]))
     pl.semaphore_wait(barrier, owners - 1)
     spread(first, 0)
+    toks = owner_of.shape[1]
+    before = lax.broadcasted_iota(jnp.int32, (toks, toks), 0)
+    after = lax.broadcasted_iota(jnp.int32, (toks, toks), 1)
+    owner = owner_of[...]
+    owner_column = jnp.sum(jnp.where(before == after, owner, 0), axis=1, keepdims=True)
+    same = (owner_column == owner) & (before < after)
+    rank = jnp.sum(jnp.where(same, 1, 0), axis=0, keepdims=True)
+    slots = lax.broadcasted_iota(jnp.int32, (owners * SUBLANES, toks), 0)
+    placing[...] = jnp.where(slots == owner * SUBLANES + rank, 1.0, 0.0).astype(jnp.bfloat16)
     weight_copy.wait()
-    for layer in range(2):
-        for tap in range(27):
-            group, e = tap // 3, tap % 3
-            taps[layer, group, e * out : (e + 1) * out] = raw[layer, :, tap, :]
     hidden = convolve(first, 0)
     keep(second, norm_silu(hidden, gains[1:2]))
     spread(second, 1)
     hidden = convolve(second, 1)
     merged = feat[...].reshape(cells, width).astype(jnp.float32) + hidden
     active = norm_silu(merged, gains[2:3]).astype(jnp.bfloat16)
-    latent = jnp.dot(active, latent_wide[...], preferred_element_type=jnp.float32)
+    rest = jnp.zeros((LANES - 4 * width_latent, width), jnp.bfloat16)
+    latent_wide = jnp.concatenate([latent_rows[...]] * 4 + [rest], axis=0)
+    latent = lax.dot_general(
+        active, latent_wide, (((1,), (1,)), ((), ())), preferred_element_type=jnp.float32
+    )
     cell = lax.broadcasted_iota(jnp.int32, (cells, LANES), 0)
     lane = lax.broadcasted_iota(jnp.int32, (cells, LANES), 1)
     corner = (cell // cols % 2) * 2 + cell % 2
     alive = (t * frames + cell // (rows * cols) < count[0]) & (corner == 0)
     flagged = jnp.where((lane == 4 * width_latent) & alive, 1.0, 0.0)
     patches = jnp.where(lane // width_latent == corner, latent, flagged).astype(jnp.bfloat16)
-    slots = lax.broadcasted_iota(jnp.int32, (owners * SUBLANES, cells), 0)
-    placing = jnp.where(slots == targets[...], 1.0, 0.0).astype(jnp.bfloat16)
-    outgoing = jnp.dot(placing, patches, preferred_element_type=jnp.float32).astype(jnp.bfloat16)
+    spot = lax.broadcasted_iota(jnp.int32, (toks, cells), 1)
+    patch = (spot // (2 * cols)) * (cols // 2) + spot % cols // 2
+    mine = patch == lax.broadcasted_iota(jnp.int32, (toks, cells), 0)
+    patches = jnp.dot(
+        jnp.where(mine, 1.0, 0.0).astype(jnp.bfloat16), patches, preferred_element_type=jnp.float32
+    ).astype(jnp.bfloat16)
+    outgoing = jnp.dot(
+        placing[...], patches, preferred_element_type=jnp.float32
+    ).astype(jnp.bfloat16)
     tok_out[...] = outgoing.reshape(owners, SUBLANES, LANES)
     tok_in[pl.ds(me, 1)] = tok_out[pl.ds(me, 1)]
 
@@ -275,6 +290,13 @@
         preferred_element_type=jnp.float32,
     ).astype(jnp.bfloat16)
     lax.fori_loop(1, owners, tok_sent, 0)
+
+
+def embedder(channels, tokens, weight, bias, packed):
+    held = tokens[...]
+    projected = jnp.dot(held[:, :channels], weight[...], preferred_element_type=jnp.float32)
+    flags = held[:, channels : channels + 1].astype(jnp.float32)
+    packed[...] = ((projected + bias[...]) * flags).astype(jnp.bfloat16)
 
 
 def shards(
@@ -298,17 +320,6 @@
     latents = latent_weight.shape[1]
     tok_count = routes.shape[1]
     most = (tok_count + owners - 1) // owners + 1
-    destinations = routes[0, :, 0]
-    positions = jnp.arange(tok_count, dtype=jnp.int32)
-    before = positions[:, None] > positions[None, :]
-    ranks = jnp.sum(
-        ((destinations[:, None] == destinations[None, :]) & before).astype(jnp.int32), axis=1
-    )
-    slots = (destinations * SUBLANES + ranks).reshape(frames, rows // 2, 1, cols // 2, 1)
-    targets = jnp.broadcast_to(slots, (frames, rows // 2, 2, cols // 2, 2)).reshape(1, cells)
-    latent_wide = jnp.pad(
-        jnp.concatenate([latent_weight] * 4, axis=1), ((0, 0), (0, LANES - 4 * latents))
-    )
     vmem = pl.BlockSpec(memory_space=pltpu.VMEM)
     dma = pltpu.SemaphoreType.DMA
     field = pltpu.VMEM((n * frames + 2, rows + 2, cols, width), jnp.bfloat16)
@@ -322,20 +333,38 @@
         out_specs=vmem,
         scratch_shapes=[
             field, field,
-            pltpu.VMEM(conv_weights.shape, jnp.bfloat16),
             pltpu.VMEM((2, 9, 3 * out, width), jnp.bfloat16),
+            pltpu.VMEM((owners * SUBLANES, tok_count), jnp.bfloat16),
             slab, slab, tok, tok,
             dma,
             dma((2, n)), dma((2, n)), dma((2, n)), dma((2, n)), dma((2, n)), dma((2, n)),
             dma((2, n)), dma((2, n)), dma((owners,)), dma((owners,)),
         ],
         compiler_params=pltpu.CompilerParams(collective_id=0, has_side_effects=True),
-    )(feat, conv_weights, norm_gains, conv_biases, latent_wide, targets, frame_counts)
+    )(
+        feat,
+        conv_weights.transpose(0, 2, 1, 3).reshape(2, 9, 3 * out, width),
+        norm_gains,
+        conv_biases,
+        latent_weight.T,
+        routes.reshape(1, tok_count),
+        frame_counts,
+    )
     channels = 4 * latents
-    projected = (
-        jnp.dot(tokens[:, :channels], embed_weight, preferred_element_type=jnp.float32) + embed_bias
-    ) * tokens[:, channels : channels + 1].astype(jnp.float32)
-    return projected.astype(jnp.bfloat16)[None]
+    embed = embed_weight.shape[1]
+    chunk = embed // 3 if embed % (3 * LANES) == 0 else embed
+    packed = pl.pallas_call(
+        functools.partial(embedder, channels),
+        grid=(embed // chunk,),
+        out_shape=jax.ShapeDtypeStruct((owners * most, embed), jnp.bfloat16),
+        in_specs=[
+            pl.BlockSpec((owners * most, LANES), lambda i: (0, 0)),
+            pl.BlockSpec((channels, chunk), lambda i: (0, i)),
+            pl.BlockSpec((1, chunk), lambda i: (0, i)),
+        ],
+        out_specs=pl.BlockSpec((owners * most, chunk), lambda i: (0, i)),
+    )(tokens, embed_weight, embed_bias.reshape(1, embed))
+    return packed[None]
 
 
 def solution(mesh):

time: 66.4 us -> 58.4 us (0.88)
  local copies, waits for them, and re-layouts: 5.67 us -> 0 us
  other arithmetic: 3.25 us -> 0 us
  Pallas kernels: 54.6 us -> 57.6 us
  matrix products: 1.76 us -> 0 us
    unnamed x6 -> x0, local copies, waits for them, and re-layouts: 4.68 us -> none
    pallas_call x0 -> x1, Pallas kernels: none -> 2.91 us  [shards(): pl.pallas_call(functools.partial(embedder, channels), grid=(embed // chun...]
    dot_general x1 -> x0, matrix products: 1.76 us -> none  [shards(): jnp.dot(tokens[:, :channels], embed_weight, preferred_element_type=jnp.fl...]
    mul x2 -> x0, other arithmetic: 1.58 us -> none  [the longest x1 0.9 us: shards(): (jnp.dot(tokens[:, :channels], embed_weight, preferred_element_type=jnp.f...]
    reduce_sum x1 -> x0, other arithmetic: 0.91 us -> none  [shards(): jnp.sum(((destinations[:, None] == destinations[None, :]) & before).astyp...]
    concatenate x1 -> x0, other arithmetic: 0.76 us -> none  [shards(): jnp.concatenate([latent_weight] * 4, axis=1)]
    reshape x1 -> x0, local copies, waits for them, and re-layouts: 0.75 us -> none  [shards(): jnp.broadcast_to(slots, (frames, rows // 2, 2, cols // 2, 2))]
where the time goes in v2:
time: 58.4 us; the launch traced here: 58.3 us
  Pallas kernels  57.6 us (99%)
  between operations  0.66 us (1%)
    pallas_call x1, Pallas kernels, shards(): pl.pallas_call(functools.partial(encoder, n, ns, most, latents), out_shap...  54.7 us
    pallas_call x1, Pallas kernels, shards(): pl.pallas_call(functools.partial(embedder, channels), grid=(embed // chun...  2.91 us

profile of v2, /device:TPU:0, one launch (start us, length us, event | category | flops | bytes accessed | tf_op | source)
XLA Modules:
  0.0 58.3 jit_solution(9588878012823441533)
XLA Ops:
  0.7 54.7 %shard_map.91.tokens = bf16[72,128]{1,0:T(8,128)(2,1)} custom-call(bf16[4,4,16,256]{3,2,1,0:T(8,128)(2,1)} %bitcast.9, bf16[2,9,192,256]{3,2,1,0:T(8,128)(2,1)} %bitcast.8, f32[3,256]{1,0:T(4,128)} %gains.1, f32[2,256]{1,0:T(2,128)} %biases.1, bf16[16,256]{1,0:T(8,128)(2,1)} %bitcast.11, s32[1,64]{1,0:T(1,128)} %bitcast.12, s32[1]{0:T(128)S(6)} %copy.10.count), custom_call_target="tpu_custom_call" | custom-call | tf_op jit(solution)/shard_map/pallas_call | solution.py:328
  55.4 2.9 %shard_map.92 = bf16[72,3072]{1,0:T(8,128)(2,1)} custom-call(bf16[72,128]{1,0:T(8,128)(2,1)} %shard_map.91.tokens, bf16[64,3072]{1,0:T(8,128)(2,1)} %weight.1, f32[1,3072]{1,0:T(1,128)} %bitcast.10), custom_call_target="tpu_custom_call" | custom-call | tf_op jit(solution)/shard_map/pallas_call | solution.py:356

commit v3 on v2

--- a/solution.py
+++ b/solution.py
@@ -10,6 +10,7 @@
 MESH = pl.DeviceIdType.MESH
 LANES = 128
 SUBLANES = 16
+CUTS = 2
 
 
 def norm_silu(values, gain):
@@ -33,9 +34,10 @@
     frames, rows, cols, width = feat.shape
     cells = frames * rows * cols
     out = weights_any.shape[2] // 3
+    cuts = block_recv.shape[2]
+    size = frames // cuts
     pack = max(1, LANES // out)
     part = cells // pack
-    step = jnp.where(t < n // 2, 1, -1)
 
     barrier = pltpu.get_barrier_semaphore()
 
@@ -68,28 +70,28 @@
             frames, rows, cols, width
         )
 
-    def block_copy(buf, layer, source, target):
-        span = buf.at[pl.ds(2 + frames * source, frames), pl.ds(1, rows)]
+    def block_copy(buf, layer, c, f, way):
+        span = buf.at[pl.ds(2 + frames * c + size * f, size), pl.ds(1, rows)]
         return pltpu.make_async_remote_copy(
             src_ref=span, dst_ref=span,
-            send_sem=block_send.at[layer, target], recv_sem=block_recv.at[layer, source],
-            device_id={"tm": target}, device_id_type=MESH,
-        )
-
-    def up_copy(buf, layer, source, target, side):
-        return pltpu.make_async_remote_copy(
-            src_ref=buf.at[pl.ds(2 + frames * source, frames), pl.ds(1, 1)],
-            dst_ref=buf.at[pl.ds(2 + frames * source, frames), pl.ds(rows + 1, 1)],
-            send_sem=up_send.at[layer, target], recv_sem=up_recv.at[layer, source],
-            device_id={"tm": target, "space": side}, device_id_type=MESH,
-        )
-
-    def down_copy(buf, layer, source, target, side):
-        return pltpu.make_async_remote_copy(
-            src_ref=buf.at[pl.ds(2 + frames * source, frames), pl.ds(rows, 1)],
-            dst_ref=buf.at[pl.ds(2 + frames * source, frames), pl.ds(0, 1)],
-            send_sem=down_send.at[layer, target], recv_sem=down_recv.at[layer, source],
-            device_id={"tm": target, "space": side}, device_id_type=MESH,
+            send_sem=block_send.at[layer, way, c, f], recv_sem=block_recv.at[layer, c, f],
+            device_id={"tm": (t + 1 - 2 * way + n) % n}, device_id_type=MESH,
+        )
+
+    def up_copy(buf, layer, c, f):
+        return pltpu.make_async_remote_copy(
+            src_ref=buf.at[pl.ds(2 + frames * c + size * f, size), pl.ds(1, 1)],
+            dst_ref=buf.at[pl.ds(2 + frames * c + size * f, size), pl.ds(rows + 1, 1)],
+            send_sem=up_send.at[layer, c, f], recv_sem=up_recv.at[layer, c, f],
+            device_id={"space": (s + ns - 1) % ns}, device_id_type=MESH,
+        )
+
+    def down_copy(buf, layer, c, f):
+        return pltpu.make_async_remote_copy(
+            src_ref=buf.at[pl.ds(2 + frames * c + size * f, size), pl.ds(rows, 1)],
+            dst_ref=buf.at[pl.ds(2 + frames * c + size * f, size), pl.ds(0, 1)],
+            send_sem=down_send.at[layer, c, f], recv_sem=down_recv.at[layer, c, f],
+            device_id={"space": (s + 1) % ns}, device_id_type=MESH,
         )
 
     def slab_copy(layer, source, target):
@@ -99,78 +101,42 @@
             device_id={"tm": target}, device_id_type=MESH,
         )
 
+    def outward(buf, layer, c, f, act):
+        pl.when((c <= t) & (t < n - 1))(lambda: act(block_copy(buf, layer, c, f, 0)))
+        pl.when((c >= t) & (t > 0))(lambda: act(block_copy(buf, layer, c, f, 1)))
+        pl.when(s > 0)(lambda: act(up_copy(buf, layer, c, f)))
+        pl.when(s < ns - 1)(lambda: act(down_copy(buf, layer, c, f)))
+
     def spread(buf, layer):
-        def send(k, carry):
-            target = (t + k * step + n) % n
-
-            @pl.when(k > 0)
+        for f in range(cuts):
+            outward(buf, layer, t, f, lambda copy: copy.start())
+
+    def spread_sent(buf, layer):
+        def sent(c, carry):
+            for f in range(cuts):
+                outward(buf, layer, c, f, lambda copy: copy.wait_send())
+
+            @pl.when(c != t)
             def _():
-                block_copy(buf, layer, t, target).start()
-
-            @pl.when(s > 0)
-            def _():
-                up_copy(buf, layer, t, target, s - 1).start()
-
-            @pl.when(s < ns - 1)
-            def _():
-                down_copy(buf, layer, t, target, s + 1).start()
+                slab_copy(layer, t, c).wait_send()
 
             return carry
 
-        lax.fori_loop(0, n, send, 0)
-
-    def spread_sent(buf, layer):
-        def sent(k, carry):
-            target = (t + k * step + n) % n
-
-            @pl.when(k > 0)
-            def _():
-                block_copy(buf, layer, t, target).wait_send()
-                slab_copy(layer, t, target).wait_send()
-
-            @pl.when(s > 0)
-            def _():
-                up_copy(buf, layer, t, target, s - 1).wait_send()
-
-            @pl.when(s < ns - 1)
-            def _():
-                down_copy(buf, layer, t, target, s + 1).wait_send()
-
-            return carry
-
         lax.fori_loop(0, n, sent, 0)
 
-    def arrive(buf, layer, c):
-        @pl.when(c != t)
-        def _():
-            block_copy(buf, layer, c, c).wait_recv()
-
-        @pl.when(s < ns - 1)
-        def _():
-            up_copy(buf, layer, c, c, s + 1).wait_recv()
-
-        @pl.when(s > 0)
-        def _():
-            down_copy(buf, layer, c, c, s - 1).wait_recv()
+    def handle(buf, layer, c, f):
+        block_copy(buf, layer, c, f, 0).wait_recv()
+        outward(buf, layer, c, f, lambda copy: copy.start())
+
+    def rims(buf, layer, c):
+        for f in range(cuts):
+            pl.when(s < ns - 1)(lambda: up_copy(buf, layer, c, f).wait_recv())
+            pl.when(s > 0)(lambda: down_copy(buf, layer, c, f).wait_recv())
 
     column = lax.broadcasted_iota(jnp.int32, (cells, 1), 0) % cols
 
     def convolve(buf, layer):
-        def place(b):
-            return ((b - t) * step + n) % n
-
-        def one(k, carry):
-            b = (t + k * step + n) % n
-            here = place(b)
-
-            @pl.when((b == n - 1) | (place((b + 1) % n) > here))
-            def _():
-                arrive(buf, layer, b)
-
-            @pl.when((b > 0) & (place((b + n - 1) % n) > here))
-            def _():
-                arrive(buf, layer, (b + n - 1) % n)
-
+        def one(b):
             total = jnp.zeros((cells, 3 * out), jnp.float32)
             for a in range(3):
                 for r in range(3):
@@ -195,9 +161,25 @@
                 slab_out[layer, pl.ds(b, 1)] = packed[None]
                 slab_copy(layer, t, b).start()
 
+        def ring(d, carry):
+            low, high = t - d, t + d
+            is_low, is_high = low >= 0, high < n
+            for f in range(cuts):
+                pl.when(is_low)(lambda: handle(buf, layer, (low + n) % n, f))
+                pl.when(is_high)(lambda: handle(buf, layer, high % n, f))
+            pl.when(d == 1)(lambda: rims(buf, layer, t))
+            pl.when(is_low)(lambda: rims(buf, layer, (low + n) % n))
+            pl.when(is_high)(lambda: rims(buf, layer, high % n))
+
+            def ready(i, carry):
+                b = jnp.where(i == 0, low + 1, high)
+                pl.when((b >= 0) & (b < n))(lambda: one((b + n) % n))
+                return carry
+
+            lax.fori_loop(0, 2, ready, 0)
             return carry
 
-        lax.fori_loop(0, n, one, 0)
+        lax.fori_loop(1, n + 1, ring, 0)
 
         def came(k, carry):
             slab_copy(layer, (t + k) % n, (t + k) % n).wait_recv()
@@ -215,8 +197,6 @@
         return hidden + biases[layer : layer + 1]
 
     keep(first, norm_silu(inputs, gains[0:1]))
-    pl.semaphore_wait(barrier, owners - 1)
-    spread(first, 0)
     toks = owner_of.shape[1]
     before = lax.broadcasted_iota(jnp.int32, (toks, toks), 0)
     after = lax.broadcasted_iota(jnp.int32, (toks, toks), 1)
@@ -226,6 +206,8 @@
     rank = jnp.sum(jnp.where(same, 1, 0), axis=0, keepdims=True)
     slots = lax.broadcasted_iota(jnp.int32, (owners * SUBLANES, toks), 0)
     placing[...] = jnp.where(slots == owner * SUBLANES + rank, 1.0, 0.0).astype(jnp.bfloat16)
+    pl.semaphore_wait(barrier, owners - 1)
+    spread(first, 0)
     weight_copy.wait()
     hidden = convolve(first, 0)
     keep(second, norm_silu(hidden, gains[1:2]))
@@ -324,6 +306,7 @@
     dma = pltpu.SemaphoreType.DMA
     field = pltpu.VMEM((n * frames + 2, rows + 2, cols, width), jnp.bfloat16)
     slab = pltpu.VMEM((2, n, cells // pack, pack * out), jnp.bfloat16)
+    cuts = CUTS if frames % CUTS == 0 else 1
     tok = pltpu.VMEM((owners, SUBLANES, LANES), jnp.bfloat16)
     tokens = pl.pallas_call(
         functools.partial(encoder, n, ns, most, latents),
@@ -337,7 +320,8 @@
             pltpu.VMEM((owners * SUBLANES, tok_count), jnp.bfloat16),
             slab, slab, tok, tok,
             dma,
-            dma((2, n)), dma((2, n)), dma((2, n)), dma((2, n)), dma((2, n)), dma((2, n)),
+            dma((2, 2, n, cuts)), dma((2, n, cuts)), dma((2, n, cuts)), dma((2, n, cuts)),
+            dma((2, n, cuts)), dma((2, n, cuts)),
             dma((2, n)), dma((2, n)), dma((owners,)), dma((owners,)),
         ],
         compiler_params=pltpu.CompilerParams(collective_id=0, has_side_effects=True),
@@ -352,7 +336,7 @@
     )
     channels = 4 * latents
     embed = embed_weight.shape[1]
-    chunk = embed // 3 if embed % (3 * LANES) == 0 else embed
+    chunk = embed // 1 if embed % (1 * LANES) == 0 else embed
     packed = pl.pallas_call(
         functools.partial(embedder, channels),
         grid=(embed // chunk,),

time: 58.4 us -> 56.9 us (0.974)
  Pallas kernels: 57.6 us -> 56.1 us
    pallas_call x1, Pallas kernels: 2.91 us -> 2.03 us  [shards(): pl.pallas_call(functools.partial(embedder, channels), grid=(embed // chun...]
    pallas_call x1, Pallas kernels: 54.7 us -> 54.1 us  [shards(): pl.pallas_call(functools.partial(encoder, n, ns, most, latents), out_shap...]
where the time goes in v3:
time: 56.9 us; the launch traced here: 56.8 us
  Pallas kernels  56.1 us (99%)
  between operations  0.66 us (1%)
    pallas_call x1, Pallas kernels, shards(): pl.pallas_call(functools.partial(encoder, n, ns, most, latents), out_shap...  54.1 us
    pallas_call x1, Pallas kernels, shards(): pl.pallas_call(functools.partial(embedder, channels), grid=(embed // chun...  2.03 us

profile of v3, /device:TPU:0, one launch (start us, length us, event | category | flops | bytes accessed | tf_op | source)
XLA Modules:
  0.0 56.8 jit_solution(17735057878321155054)
XLA Ops:
  0.7 54.1 %shard_map.91.tokens = bf16[72,128]{1,0:T(8,128)(2,1)} custom-call(bf16[4,4,16,256]{3,2,1,0:T(8,128)(2,1)} %bitcast.9, bf16[2,9,192,256]{3,2,1,0:T(8,128)(2,1)} %bitcast.8, f32[3,256]{1,0:T(4,128)} %gains.1, f32[2,256]{1,0:T(2,128)} %biases.1, bf16[16,256]{1,0:T(8,128)(2,1)} %bitcast.11, s32[1,64]{1,0:T(1,128)} %bitcast.12, s32[1]{0:T(128)S(6)} %copy.10.count), custom_call_target="tpu_custom_call" | custom-call | tf_op jit(solution)/shard_map/pallas_call | solution.py:311
  54.7 2.0 %shard_map.92 = bf16[72,3072]{1,0:T(8,128)(2,1)} custom-call(bf16[72,128]{1,0:T(8,128)(2,1)} %shard_map.91.tokens, bf16[64,3072]{1,0:T(8,128)(2,1)} %weight.1, f32[1,3072]{1,0:T(1,128)} %bitcast.10), custom_call_target="tpu_custom_call" | custom-call | tf_op jit(solution)/shard_map/pallas_call | solution.py:340

commit v4 on v3

--- a/solution.py
+++ b/solution.py
@@ -10,7 +10,7 @@
 MESH = pl.DeviceIdType.MESH
 LANES = 128
 SUBLANES = 16
-CUTS = 2
+CUTS = 4
 
 
 def norm_silu(values, gain):
@@ -167,19 +167,21 @@
             for f in range(cuts):
                 pl.when(is_low)(lambda: handle(buf, layer, (low + n) % n, f))
                 pl.when(is_high)(lambda: handle(buf, layer, high % n, f))
-            pl.when(d == 1)(lambda: rims(buf, layer, t))
+            low, high = low + 1, high - 1
+            is_low, is_high = (low >= 0) & (low < t), (high < n) & (high > t)
+            pl.when(d == 2)(lambda: rims(buf, layer, t))
             pl.when(is_low)(lambda: rims(buf, layer, (low + n) % n))
             pl.when(is_high)(lambda: rims(buf, layer, high % n))
 
             def ready(i, carry):
-                b = jnp.where(i == 0, low + 1, high)
-                pl.when((b >= 0) & (b < n))(lambda: one((b + n) % n))
+                b = jnp.where(i == 0, high, low + 1)
+                pl.when((d > 1) & (b >= 0) & (b < n))(lambda: one((b + n) % n))
                 return carry
 
             lax.fori_loop(0, 2, ready, 0)
             return carry
 
-        lax.fori_loop(1, n + 1, ring, 0)
+        lax.fori_loop(1, n + 2, ring, 0)
 
         def came(k, carry):
             slab_copy(layer, (t + k) % n, (t + k) % n).wait_recv()

time: 56.9 us -> 52.2 us (0.917)
  Pallas kernels: 56.1 us -> 51.4 us
    pallas_call x1, Pallas kernels: 54.1 us -> 49.4 us  [shards(): pl.pallas_call(functools.partial(encoder, n, ns, most, latents), out_shap...]
where the time goes in v4:
time: 52.2 us; the launch traced here: 52.1 us
  Pallas kernels  51.4 us (98%)
  between operations  0.66 us (1%)
    pallas_call x1, Pallas kernels, shards(): pl.pallas_call(functools.partial(encoder, n, ns, most, latents), out_shap...  49.4 us
    pallas_call x1, Pallas kernels, shards(): pl.pallas_call(functools.partial(embedder, channels), grid=(embed // chun...  2.03 us

profile of v4, /device:TPU:0, one launch (start us, length us, event | category | flops | bytes accessed | tf_op | source)
XLA Modules:
  0.0 52.1 jit_solution(14910934376203926105)
XLA Ops:
  0.7 49.4 %shard_map.91.tokens = bf16[72,128]{1,0:T(8,128)(2,1)} custom-call(bf16[4,4,16,256]{3,2,1,0:T(8,128)(2,1)} %bitcast.9, bf16[2,9,192,256]{3,2,1,0:T(8,128)(2,1)} %bitcast.8, f32[3,256]{1,0:T(4,128)} %gains.1, f32[2,256]{1,0:T(2,128)} %biases.1, bf16[16,256]{1,0:T(8,128)(2,1)} %bitcast.11, s32[1,64]{1,0:T(1,128)} %bitcast.12, s32[1]{0:T(128)S(6)} %copy.10.count), custom_call_target="tpu_custom_call" | custom-call | tf_op jit(solution)/shard_map/pallas_call | solution.py:313
  50.0 2.0 %shard_map.92 = bf16[72,3072]{1,0:T(8,128)(2,1)} custom-call(bf16[72,128]{1,0:T(8,128)(2,1)} %shard_map.91.tokens, bf16[64,3072]{1,0:T(8,128)(2,1)} %weight.1, f32[1,3072]{1,0:T(1,128)} %bitcast.10), custom_call_target="tpu_custom_call" | custom-call | tf_op jit(solution)/shard_map/pallas_call | solution.py:342
